TPU v7x, 256 devices: a whole 4x4x8 slice. The times are simulated.
256 devices in a mesh: req: 64 (over y_lo, x, z), tp: 4 (over y_hi, core).
Axes of the slice: x: 4, y: 4 (y_hi: 2, y_lo: 2; y = y_hi * 2 + y_lo), z: 8, core: 2. Of those that a mesh axis runs over, the one named last changes fastest.
Arguments:
- hidden_in: bfloat16 [128, 256, 2048], P('req', None, 'tp'), may hold values from -6 to 6
- norm_gain: float32 [2048], replicated, may hold values from 0.1 to 1.9
- q_weight: bfloat16 [2048, 2048], P(None, 'tp'), may hold values from -0.125 to 0.125
- kv_weight: bfloat16 [2048, 1024], P(None, 'tp'), may hold values from -0.125 to 0.125
- out_weight: bfloat16 [2048, 2048], P('tp'), may hold values from -3 to 3
- post_gain: float32 [2048], P('tp'), may hold values from 0.1 to 1.9
- sink_cache: bfloat16 [128, 2, 4, 512], P('req'), may hold values from -16 to 16
- window_cache: bfloat16 [128, 2, 512, 512], P('req', None, 'tp'), may hold values from -320 to 320, as said below
- cached_len: int32 [128], P('req'), may hold values from 16 to 32768, as said below
- span_len: int32 [128], P('req'), may hold values from 1 to 256, as said below
- sink_count: int32 [128], P('req'), may hold values from 1 to 4, as said below
- window_size: int32 [128], P('req'), may hold values from 128 to 512, as said below
Outputs:
- layer_out: bfloat16 [128, 256, 2048], P('req', None, 'tp')
Inputs may be any that keep to these rules, and one draw needn't show every extreme that they name: `window_cache`: slot s of request r holds the rotated key (entries below 256) and the value of position cached_len[r] - 512 + s. `cached_len`: one request has exactly 32768 cached tokens. Rows at or past span_len are padding; some request fills all 256. `sink_count`: some request keeps all 4. `window_size`: some request uses 512.
All inputs are finite; a program needn't handle non-finite values.
Results may differ from a plain program's by a relative error of at most 0.019.
Values may be sent and summed in bfloat16 or wider, within the bound.
A program may use at most 128 MiB of HBM per device.

v0:
```python
import math

import jax
import jax.numpy as jnp
from jax import lax
from jax.sharding import PartitionSpec as P

D = 2048
HEADS = 8
KVH = 2
HD = 256
WIN = 512
SINK = 4


EPS = 1e-06
NEG = -1e30


def partner(block, axis, distance):
    count = lax.axis_size(axis)
    route = []
    for low in range(count):
        high = low | 1 << distance
        if high != low and high < count:
            route += [(low, high), (high, low)]
    return lax.ppermute(block, axis, route)


def as_sent(shard):
    return jax.tree.map(lambda a: a.astype(jnp.bfloat16) if a.dtype == jnp.float32 else a, shard)


def rotate(block_rows, positions):
    half_size = block_rows.shape[-1] // 2
    frequency = jnp.exp(
        jnp.arange(half_size, dtype=jnp.float32) * (-2.0 * math.log(10000.0) / block_rows.shape[-1])
    )
    angles = positions.astype(jnp.float32)[..., None] * frequency
    cosine = jnp.cos(angles)[..., None, :]
    sine_part = jnp.sin(angles)[..., None, :]
    first_half = block_rows[..., :half_size]
    second_half = block_rows[..., half_size:]
    return jnp.concatenate(
        [
            first_half * cosine - second_half * sine_part,
            second_half * cosine + first_half * sine_part,
        ],
        axis=-1,
    )


def join_partials(left_part, right_part):
    peak_max = jnp.maximum(left_part[0], right_part[0])
    left_factor = jnp.exp(left_part[0] - peak_max)
    right_factor = jnp.exp(right_part[0] - peak_max)
    row_total = left_part[1] * left_factor + right_part[1] * right_factor
    weighted = left_part[2] * left_factor[..., None] + right_part[2] * right_factor[..., None]
    return (peak_max, row_total, weighted)


def attend(
    query_rows,
    keys,
    values,
    key_pos,
    key_ok,
    windowed,
    query_pos,
    reach_len,
    start_block,
    block_size,
):
    requests, span_rows, kv_heads, groups = (
        query_rows.shape[0],
        query_rows.shape[1],
        query_rows.shape[2],
        query_rows.shape[3],
    )
    scaling = 1.0 / math.sqrt(query_rows.shape[4])
    block_total = keys.shape[2] // block_size
    row_max = jnp.full((requests, kv_heads, groups, span_rows), NEG, jnp.float32)
    row_total = jnp.zeros((requests, kv_heads, groups, span_rows), jnp.float32)
    weighted = jnp.zeros((requests, kv_heads, groups, span_rows, query_rows.shape[4]), jnp.float32)

    def step(block_id, carry):
        run_max, run_total, run_sum = carry
        pos_gap = query_pos[:, :, None] - key_pos[:, None, :]
        inside = (pos_gap >= 0) & (pos_gap < reach_len[:, None, None])
        allowed = key_ok[:, None, :] & (jnp.logical_not(windowed)[:, None, :] | inside)
        key_mask = allowed[:, None, None, :, :]
        scores = (
            jnp.einsum("rcvgd,rvbd->rvgcb", query_rows, keys, preferred_element_type=jnp.float32)
            * scaling
        )
        scores = jnp.where(key_mask, scores, NEG)
        new_max = jnp.maximum(run_max, jnp.max(scores, axis=-1))
        weights = jnp.where(key_mask, jnp.exp(scores - new_max[..., None]), 0.0)
        factor = jnp.exp(run_max - new_max)
        new_total = run_total * factor + jnp.sum(weights, axis=-1)
        new_sum = run_sum * factor[..., None] + jnp.einsum(
            "rvgcb,rvbd->rvgcd",
            weights.astype(jnp.bfloat16),
            values,
            preferred_element_type=jnp.float32,
        )
        return (new_max, new_total, new_sum)

    return lax.fori_loop(start_block, block_total, step, (row_max, row_total, weighted))


def first_block(cached, sinks_kept, reach_len, first_slot, slot_total, block_size):
    first_live = jnp.maximum(sinks_kept, cached - reach_len + 1) - (cached - WIN + first_slot)
    return jnp.min(jnp.clip(first_live, 0, slot_total)) // block_size


def window_part(query_rows, cache_rows, cached, sinks_kept, reach_len, first_slot, slot_total):
    span_rows = query_rows.shape[1]
    query_pos = cached[:, None] + jnp.arange(span_rows, dtype=jnp.int32)[None, :]
    slot_pos = cached[:, None] - WIN + first_slot + jnp.arange(slot_total, dtype=jnp.int32)[None, :]
    slot_ok = slot_pos >= sinks_kept[:, None]
    windowed = jnp.ones_like(slot_ok)
    block_size = math.gcd(slot_total, 256)
    start_block = first_block(cached, sinks_kept, reach_len, first_slot, slot_total, block_size)
    return attend(
        query_rows,
        cache_rows[..., :HD],
        cache_rows[..., HD:],
        slot_pos,
        slot_ok,
        windowed,
        query_pos,
        reach_len,
        start_block,
        block_size,
    )


def per_device(
    hidden_in,
    norm_gain,
    q_weight,
    kv_weight,
    out_weight,
    post_gain,
    sink_cache,
    window_cache,
    cached_len,
    span_len,
    sink_count,
    window_size,
):
    tp_rank = lax.axis_index("tp")
    tp_count = lax.axis_size("tp")
    groups = HEADS // KVH
    gathered = lax.all_gather(hidden_in, "tp", axis=2, tiled=True)
    requests, span_rows = (gathered.shape[0], gathered.shape[1])
    widened = gathered.astype(jnp.float32)
    normed = (
        widened * lax.rsqrt(jnp.mean(widened * widened, axis=-1, keepdims=True) + EPS) * norm_gain
    ).astype(jnp.bfloat16)
    row_index = jnp.arange(span_rows, dtype=jnp.int32)
    positions = cached_len[:, None] + row_index[None, :]
    local_heads = q_weight.shape[1] // HD
    query_part = jnp.einsum(
        "rcd,dk->rck", normed, q_weight, preferred_element_type=jnp.float32
    ).reshape(requests, span_rows, local_heads, HD)
    query_part = (
        rotate(query_part, positions)
        .astype(jnp.bfloat16)
        .reshape(requests, span_rows, local_heads * HD)
    )
    kv_blocks = kv_weight.shape[1] // HD
    pair_part = jnp.einsum(
        "rcd,dk->rck", normed, kv_weight, preferred_element_type=jnp.float32
    ).reshape(requests, span_rows, kv_blocks, HD)
    block_ids = tp_rank * kv_blocks + jnp.arange(kv_blocks, dtype=jnp.int32)
    is_key = (block_ids % 2 == 0)[None, None, :, None]
    pair_part = (
        jnp.where(is_key, rotate(pair_part, positions), pair_part)
        .astype(jnp.bfloat16)
        .reshape(requests, span_rows, kv_blocks * HD)
    )
    queries, fresh_pairs = (
        lax.all_gather(query_part, "tp", axis=2, tiled=True),
        lax.all_gather(pair_part, "tp", axis=2, tiled=True),
    )
    queries = queries.reshape(requests, span_rows, KVH, groups, HD)
    fresh_pairs = fresh_pairs.reshape(requests, span_rows, KVH, 2, HD)
    share_rows = span_rows // tp_count
    start_row = tp_rank * share_rows
    fresh_share = lax.dynamic_slice_in_dim(fresh_pairs, start_row, share_rows, 1)
    fresh_keys = jnp.transpose(fresh_share[:, :, :, 0, :], (0, 2, 1, 3))
    fresh_values = jnp.transpose(fresh_share[:, :, :, 1, :], (0, 2, 1, 3))
    extra_keys = jnp.concatenate([sink_cache[..., :HD], fresh_keys], axis=2)
    extra_values = jnp.concatenate([sink_cache[..., HD:], fresh_values], axis=2)
    sink_index = jnp.arange(SINK, dtype=jnp.int32)
    share_index = start_row + jnp.arange(share_rows, dtype=jnp.int32)
    extra_pos = jnp.concatenate(
        [
            jnp.broadcast_to(sink_index[None, :], (requests, SINK)),
            cached_len[:, None] + share_index[None, :],
        ],
        axis=1,
    )
    extra_ok = jnp.concatenate(
        [
            (sink_index[None, :] < sink_count[:, None]) & (tp_rank == 0),
            share_index[None, :] < span_len[:, None],
        ],
        axis=1,
    )
    extra_windowed = jnp.concatenate(
        [jnp.zeros((requests, SINK), bool), jnp.ones((requests, share_rows), bool)], axis=1
    )
    extra_part = attend(
        queries,
        extra_keys,
        extra_values,
        extra_pos,
        extra_ok,
        extra_windowed,
        positions,
        window_size,
        0,
        extra_keys.shape[2],
    )
    slot_count = window_cache.shape[2]
    slot_first = tp_rank * slot_count
    half_slots = slot_count // 2
    pair_bit = lax.axis_size("req").bit_length() - 2
    own_part = window_part(
        queries,
        window_cache[:, :, half_slots:],
        cached_len,
        sink_count,
        window_size,
        slot_first + half_slots,
        half_slots,
    )
    lent_items = partner(
        (queries, window_cache[:, :, :half_slots], cached_len, sink_count, window_size),
        "req",
        pair_bit,
    )
    helped = window_part(
        lent_items[0],
        lent_items[1],
        lent_items[2],
        lent_items[3],
        lent_items[4],
        slot_first,
        half_slots,
    )
    returned = (
        partner(helped[0].astype(jnp.bfloat16), "req", pair_bit).astype(jnp.float32),
        partner(helped[1].astype(jnp.bfloat16), "req", pair_bit).astype(jnp.float32),
        partner(helped[2].astype(jnp.bfloat16), "req", pair_bit).astype(jnp.float32),
    )
    partial_value = join_partials(join_partials(own_part, extra_part), returned)
    head_total = KVH * groups
    row_max = partial_value[0].reshape(requests, head_total, span_rows)
    row_total = partial_value[1].reshape(requests, head_total, span_rows)
    weighted = partial_value[2].reshape(requests, head_total, span_rows, HD)
    from_peers = (
        lax.all_to_all(as_sent(row_max[None]), "tp", split_axis=2, concat_axis=0, tiled=True),
        lax.all_to_all(as_sent(row_total[None]), "tp", split_axis=2, concat_axis=0, tiled=True),
        lax.all_to_all(as_sent(weighted[None]), "tp", split_axis=2, concat_axis=0, tiled=True),
    )
    peak_max = jnp.max(from_peers[0], axis=0)
    factor = jnp.exp(from_peers[0] - peak_max[None])
    mine_total = jnp.sum(factor * from_peers[1], axis=0)
    mine_sum = jnp.sum(factor[..., None] * from_peers[2], axis=0)
    attended = (
        jnp.transpose(mine_sum / mine_total[..., None], (0, 2, 1, 3))
        .reshape(requests, span_rows, local_heads * HD)
        .astype(jnp.bfloat16)
    )
    terms = jnp.einsum("rck,kd->rcd", attended, out_weight, preferred_element_type=jnp.float32)
    projected = lax.psum_scatter(
        terms.astype(jnp.bfloat16), "tp", scatter_dimension=2, tiled=True
    ).astype(jnp.float32)
    square = lax.psum(jnp.sum(projected * projected, axis=-1), "tp") / D
    return (
        hidden_in.astype(jnp.float32) + post_gain * projected * lax.rsqrt(square + EPS)[..., None]
    ).astype(jnp.bfloat16)


def solution(mesh):
    in_specs = (
        P("req", None, "tp"),
        P(),
        P(None, "tp"),
        P(None, "tp"),
        P("tp", None),
        P("tp"),
        P("req", None, None, None),
        P("req", None, "tp", None),
        P("req"),
        P("req"),
        P("req"),
        P("req"),
    )
    out_specs = P("req", None, "tp")
    return jax.shard_map(
        per_device, mesh=mesh, in_specs=in_specs, out_specs=out_specs, check_vma=False
    )
```

profile of v0, /device:TPU:1, one launch (start us, length us, event | category | flops | bytes accessed | tf_op | source)
XLA Modules:
  0.0 322.6 jit_solution(1613133834305590743)
XLA Ops:
  10.4 32.2 %all-gather.4.cloned.1.call-done = bf16[2,256,2048]{2,1,0:T(8,128)(2,1)} async-done(((bf16[2,256,512]{2,1,0:T(8,128)(2,1)}), bf16[2,256,2048]{2,1,0:T(8,128)(2,1)}) %all-gather.4.cloned.1.call-update) | async-done | bytes 2097168 | tf_op jit(solution)/shard_map/all_gather | solution.py:156
  42.5 2.2 fusion.42
  44.8 3.9 %fusion.47 = f32[2,256,512]{2,1,0:T(8,128)} fusion(bf16[2048,512]{1,0:T(8,128)(2,1)} %param.18, bf16[2,256,2048]{2,1,0:T(8,128)(2,1)S(1)} %copy-done.4, f32[2048]{0:T(1024)S(1)} %copy-done.11, f32[2,256]{1,0:T(2,128)S(1)} %add_rsqrt_fusion.1), kind=kOutput, calls=%fused_computation.64 | convolution fusion | flops 1077936128 | bytes 5253120 | tf_op jit(solution)/shard_map/rcd,dk->rck/dot_general | solution.py:165
  48.7 1.9 reshape.195
  58.8 2.8 fusion.49
  63.4 19.1 %all-gather.6.cloned.1.call-done = bf16[2,256,2048]{1,2,0:T(8,128)(2,1)} async-done(((bf16[2,256,512]{1,2,0:T(8,128)(2,1)}), bf16[2,256,2048]{1,2,0:T(8,128)(2,1)}) %all-gather.6.cloned.1.call-update) | async-done | bytes 2097168 | tf_op jit(solution)/shard_map/all_gather | solution.py:185
  82.5 4.1 %copy.38 = bf16[2,256,2,4,256]{4,1,3,2,0:T(8,128)(2,1)} copy(bf16[2,256,2,4,256]{1,4,3,2,0:T(8,128)(2,1)} %bitcast.173) | data formatting | bytes 4194304 | tf_op jit(solution)/shard_map/reshape | solution.py:188
  100.7 17.8 %all-gather.8.cloned.1.call-done = bf16[2,256,1024]{1,2,0:T(8,128)(2,1)} async-done(((bf16[2,256,256]{1,2,0:T(8,128)(2,1)}), bf16[2,256,1024]{1,2,0:T(8,128)(2,1)}) %all-gather.8.cloned.1.call-update) | async-done | bytes 1048592 | tf_op jit(solution)/shard_map/all_gather | solution.py:186
  121.3 2.1 convolution_bitcast_fusion
  123.4 16.1 %collective-permute-done.3 = bf16[2,256,2,4,256]{4,1,3,2,0:T(8,128)(2,1)} collective-permute-done((bf16[2,256,2,4,256]{4,1,3,2,0:T(8,128)(2,1)}, bf16[2,256,2,4,256]{4,1,3,2,0:T(8,128)(2,1)}, u32[]{:S(2)}, u32[]{:S(2)}) %collective-permute-start.3) | collective-permute-done | bytes 2097184 | tf_op jit(solution)/shard_map/ppermute | solution.py:27
  139.5 3.3 %convolution_bitcast_fusion.1 = f32[2,2,64,256,4]{3,2,4,1,0:T(8,128)} fusion(bf16[2,256,2,4,256]{4,1,3,2,0:T(8,128)(2,1)} %collective-permute-done.3, bf16[2,2,64,512]{3,2,1,0:T(8,128)(2,1)S(1)} %collective-permute-done.4), kind=kOutput, calls=%fused_computation.71 | convolution fusion | flops 134217728 | bytes 3276800 | tf_op jit(solution)/shard_map/while/body/rcvgd,rvbd->rvgcb/dot_general | solution.py:93
  142.8 2.4 broadcast.272.clone
  145.2 9.4 %while.43 = (s32[]{:T(128)}, f32[2,2,4,256]{3,2,1,0:T(4,128)S(1)}, f32[2,2,4,256]{3,2,1,0:T(4,128)S(1)}, f32[2,2,4,256,256]{4,3,2,1,0:T(8,128)}, s32[2]{0:T(128)...) while((s32[]{:T(128)}, f32[2,2,4,256]{3,2,1,0:T(4,128)S(1)}, ...), condition=%wide.region_11.12_spmd.clone.clone, body=%wide.region_8.11_spmd.clone.clone.sunk | while | flops 139895680 | bytes 16258481 | solution.py:109
  150.5 4.1 %multiply_add_fusion.11 = f32[2,2,4,256,256]{4,3,2,1,0:T(8,128)} fusion(f32[2,2,4,256,256]{4,3,2,1,0:T(8,128)} %get-tuple-element.630, f32[2,2,4,256]{3,2,1,0:T(4,128)S(1)} %bitcast.183, f32[2,2,64,256,4]{3,2,4,1,0:T(8,128)S(1)} %copy-done.1, f32[2,2,4,256]{3,2,1,0:T(4,128)S(1)} %max.113, pred[2,256,64]{1,2,0:T(8,128)(4,1)S(1)} %fusion.121, ...), kind=kOutput, calls=%fused_computation.30.clone.1 | convolution fusion | flops 137625600 | bytes 9633792 | tf_op jit(solution)/shard_map/while/body/rvgcb,rvbd->rvgcd/dot_general | solution.py:101
  154.6 3.8 %convert_element_type.124 = bf16[2,2,4,256,256]{4,3,2,1,0:T(8,128)(2,1)} convert(f32[2,2,4,256,256]{4,3,2,1,0:T(8,128)} %get-tuple-element.293) | non-fusion elementwise | flops 1048576 | bytes 6291456 | tf_op jit(solution)/shard_map/convert_element_type | solution.py:258
  158.7 2.4 broadcast.272.clone.1
  161.1 6.9 %while.42 = (s32[]{:T(128)}, f32[2,2,4,256]{3,2,1,0:T(4,128)S(1)}, f32[2,2,4,256]{3,2,1,0:T(4,128)S(1)}, f32[2,2,4,256,256]{4,3,2,1,0:T(8,128)}, s32[2]{0:T(128)...) while((s32[]{:T(128)}, f32[2,2,4,256]{3,2,1,0:T(4,128)S(1)}, ...), condition=%wide.region_5.6_spmd.clone.clone, body=%wide.region_2.5_spmd.clone.clone.sunk | while | flops 139895680 | bytes 12064149 | solution.py:109
  163.9 4.1 %multiply_add_fusion.9 = f32[2,2,4,256,256]{4,3,2,1,0:T(8,128)} fusion(f32[2,2,4,256,256]{4,3,2,1,0:T(8,128)} %get-tuple-element.663, f32[2,2,4,256]{3,2,1,0:T(4,128)S(1)} %bitcast.184, f32[2,2,64,256,4]{3,2,4,1,0:T(8,128)S(1)} %get-tuple-element.676, f32[2,2,4,256]{3,2,1,0:T(4,128)S(1)} %max.112, pred[2,256,64]{1,2,0:T(8,128)(4,1)S(1)} %fusion.116, ...), kind=kOutput, calls=%fused_computation.6.clone.1 | convolution fusion | flops 137625600 | bytes 9633792 | tf_op jit(solution)/shard_map/while/body/rvgcb,rvbd->rvgcd/dot_general | solution.py:101
  168.0 2.2 fusion.99
  170.3 2.7 fusion.61
  174.9 23.6 %collective-permute-done.7 = bf16[2,2,4,256]{3,2,1,0:T(4,128)(2,1)S(1)} collective-permute-done((bf16[2,2,4,256]{3,2,1,0:T(4,128)(2,1)S(1)}, bf16[2,2,4,256]{3,2,1,0:T(4,128)(2,1)S(1)}, u32[]{:S(2)}, u32[]{:S(2)}) %collective-permute-start.7) | collective-permute-done | bytes 8224 | tf_op jit(solution)/shard_map/ppermute | solution.py:27
  199.2 10.9 %all-to-all-start.2 = ((bf16[1,2,8,256]{3,1,0,2:T(2,128)(2,1)}), bf16[1,2,8,256]{3,1,0,2:T(2,128)(2,1)S(1)}, u32[]{:S(2)}, u32[]{:S(2)}) async-start(bf16[1,2,8,256]{3,1,0,2:T(2,128)(2,1)} %bitcast.34), calls=%async_computation.2 | async-start | bytes 16384 | tf_op jit(solution)/shard_map/all_to_all | solution.py:267
  210.7 4.0 %all-to-all-done.2 = bf16[1,2,8,256]{3,1,0,2:T(2,128)(2,1)S(1)} async-done(((bf16[1,2,8,256]{3,1,0,2:T(2,128)(2,1)}), bf16[1,2,8,256]{3,1,0,2:T(2,128)(2,1)S(1)}, u32[]{:S(2)}, u32[]{:S(2)}) %all-to-all-start.2) | async-done | bytes 8224 | tf_op jit(solution)/shard_map/all_to_all | solution.py:267
  214.6 3.9 %all-to-all-start = ((bf16[1,2,8,256]{3,1,0,2:T(2,128)(2,1)}), bf16[1,2,8,256]{3,1,0,2:T(2,128)(2,1)S(1)}, u32[]{:S(2)}, u32[]{:S(2)}) async-start(bf16[1,2,8,256]{3,1,0,2:T(2,128)(2,1)} %bitcast.21), calls=%async_computation | async-start | bytes 16384 | tf_op jit(solution)/shard_map/all_to_all | solution.py:266
  218.6 5.9 %add_convert_fusion = bf16[2,2,4,256,256]{4,3,2,1,0:T(8,128)(2,1)S(1)} fusion(bf16[2,2,4,256,256]{4,3,2,1,0:T(8,128)(2,1)} %collective-permute-done.6, f32[2,2,4,256,256]{4,3,2,1,0:T(8,128)} %fusion.61, f32[2,2,4,256,256]{4,3,2,1,0:T(8,128)} %get-tuple-element.292, f32[2,2,4,256]{3,2,1,0:T(4,128)S(1)} %get-tuple-element.456, ...), kind=kLoop, calls=%fused_computation.59 | loop fusion | flops 9437184 | bytes 12664832 | tf_op jit(solution)/shard_map/convert_element_type | solution.py:31
  226.0 4.8 %all-to-all-start.1 = ((bf16[1,2,8,256,256]{4,3,1,0,2:T(8,128)(2,1)}), bf16[1,2,8,256,256]{4,3,1,0,2:T(8,128)(2,1)}, u32[]{:S(2)}, u32[]{:S(2)}) async-start(bf16[1,2,8,256,256]{4,3,1,0,2:T(8,128)(2,1)} %copy.41), calls=%async_computation.1 | async-start | bytes 4194304 | tf_op jit(solution)/shard_map/all_to_all | solution.py:268
  230.8 26.3 %all-to-all-done.1 = bf16[1,2,8,256,256]{4,3,1,0,2:T(8,128)(2,1)} async-done(((bf16[1,2,8,256,256]{4,3,1,0,2:T(8,128)(2,1)}), bf16[1,2,8,256,256]{4,3,1,0,2:T(8,128)(2,1)}, u32[]{:S(2)}, u32[]{:S(2)}) %all-to-all-start.1) | async-done | bytes 2097184 | tf_op jit(solution)/shard_map/all_to_all | solution.py:268
  257.1 2.1 fusion.45
  259.6 2.6 convolution_convert_fusion
  262.2 43.2 %reduce-scatter.2.cloned.1.call-done = bf16[2,256,512]{2,1,0:T(8,128)(2,1)} async-done(((bf16[2,256,2048]{2,1,0:T(8,128)(2,1)}), bf16[2,256,512]{2,1,0:T(8,128)(2,1)}) %reduce-scatter.2.cloned.1.call-update) | async-done | bytes 524304 | tf_op jit(solution)/shard_map/reduce_scatter | solution.py:280
  306.6 7.4 %psum.7 = f32[2,256]{1,0:T(2,128)S(1)} all-reduce(f32[2,256]{1,0:T(2,128)S(1)} %fusion.57), channel_id=1, replica_groups=mesh['req'=64,'tp'=4] {'tp'}, use_global_device_ids=true, to_apply=%region_18.19 | all-reduce | flops 512 | bytes 4096 | tf_op jit(solution)/shard_map/psum | solution.py:283
  314.0 2.1 fusion.56
  (117 shorter events, 40.0 us)
Async XLA Ops:
  6.5 253.1 %copy-start = (bf16[512,2048]{1,0:T(8,128)(2,1)S(1)}, bf16[512,2048]{1,0:T(8,128)(2,1)}, u32[]{:S(2)}) copy-start(bf16[512,2048]{1,0:T(8,128)(2,1)} %param.20) | copy-start | bytes 6291460
  6.5 38.2 %copy-start.11 = (f32[2048]{0:T(1024)S(1)}, f32[2048]{0:T(1024)}, u32[]{:S(2)}) copy-start(f32[2048]{0:T(1024)} %param.17) | copy-start | bytes 24580
  6.5 36.0 %all-gather.4.cloned.1.call-start = ((), (), s32[]{:S(2)}) async-start(), calls=%async_computation.4 | async-start | bytes 2621440 | tf_op jit(solution)/shard_map/all_gather | solution.py:156
  7.3 75.3 %all-gather.6.cloned.1.call-start = ((), (), s32[]{:S(2)}) async-start(), calls=%async_computation.5 | async-start | bytes 2621440 | tf_op jit(solution)/shard_map/all_gather | solution.py:185
  42.5 2.2 copy-start.4
  52.1 3.6 %copy-start.7 = (bf16[2,2,128,512]{3,2,1,0:T(8,128)(2,1)S(1)}, bf16[2,2,128,512]{3,2,1,0:T(8,128)(2,1)}, u32[]{:S(2)}) copy-start(bf16[2,2,128,512]{3,2,1,0:T(8,128)(2,1)} %param.23) | copy-start | bytes 1572868
  52.1 6.7 %copy-start.12 = (f32[2048]{0:T(1024)S(1)}, f32[2048]{0:T(1024)}, u32[]{:S(2)}) copy-start(f32[2048]{0:T(1024)} %param.17) | copy-start | bytes 24580
  53.8 64.7 %all-gather.8.cloned.1.call-start = ((), (), s32[]{:S(2)}) async-start(), calls=%async_computation.6 | async-start | bytes 1310720 | tf_op jit(solution)/shard_map/all_gather | solution.py:186
  53.8 42.5 %collective-permute-start.1 = (s32[2]{0:T(128)}, s32[2]{0:T(128)}, u32[]{:S(2)}, u32[]{:S(2)}) collective-permute-start(s32[2]{0:T(128)} %param.24), channel_id=1, source_target_pairs={{0,128},{128,0},{4,132},{132,4},{8,136},{136,8},{12,140},{140,12},... | collective-permute-start | bytes 32 | tf_op jit(solution)/shard_map/ppermute | solution.py:27
  54.2 42.1 %collective-permute-start = (s32[2]{0:T(128)}, s32[2]{0:T(128)}, u32[]{:S(2)}, u32[]{:S(2)}) collective-permute-start(s32[2]{0:T(128)} %param.26), channel_id=1, source_target_pairs={{0,128},{128,0},{4,132},{132,4},{8,136},{136,8},{12,140},{140,12},... | collective-permute-start | bytes 32 | tf_op jit(solution)/shard_map/ppermute | solution.py:27
  55.4 40.9 %collective-permute-start.2 = (s32[2]{0:T(128)}, s32[2]{0:T(128)}, u32[]{:S(2)}, u32[]{:S(2)}) collective-permute-start(s32[2]{0:T(128)} %param.27), channel_id=1, source_target_pairs={{0,128},{128,0},{4,132},{132,4},{8,136},{136,8},{12,140},{140,12},... | collective-permute-start | bytes 32 | tf_op jit(solution)/shard_map/ppermute | solution.py:27
  56.4 44.3 %collective-permute-start.4 = (bf16[2,2,64,512]{3,2,1,0:T(8,128)(2,1)}, bf16[2,2,64,512]{3,2,1,0:T(8,128)(2,1)S(1)}, u32[]{:S(2)}, u32[]{:S(2)}) collective-permute-start(bf16[2,2,64,512]{3,2,1,0:T(8,128)(2,1)} %slice.50), channel_id=1, source_target_pairs={{0,128},{128,0},{4,132},{132,4},{8,136},{136,8},{12,140},{140,12},... | collective-permute-start | bytes 786440 | tf_op jit(solution)/shard_map/ppermute | solution.py:27
  82.5 6.1 %copy-start.13 = (s32[2]{0:T(128)S(1)}, s32[2]{0:T(128)}, u32[]{:S(2)}) copy-start(s32[2]{0:T(128)} %param.25) | copy-start | bytes 28
  82.5 6.2 %copy-start.14 = (pred[2,4]{1,0:T(4,128)(4,1)S(1)}, pred[2,4]{1,0:T(4,128)(4,1)}, u32[]{:S(2)}) copy-start(pred[2,4]{1,0:T(4,128)(4,1)} %compare_and_fusion) | copy-start | bytes 28
  86.7 52.8 %collective-permute-start.3 = (bf16[2,256,2,4,256]{4,1,3,2,0:T(8,128)(2,1)}, bf16[2,256,2,4,256]{4,1,3,2,0:T(8,128)(2,1)}, u32[]{:S(2)}, u32[]{:S(2)}) collective-permute-start(bf16[2,256,2,4,256]{4,1,3,2,0:T(8,128)(2,1)} %copy.38), channel_id=1, source_target_pairs={{0,128},{128,0},{4,132},{132,4},{8,136},{136,8},{12,140},{140,12},... | collective-permute-start | bytes 6291464 | tf_op jit(solution)/shard_map/ppermute | solution.py:27
  100.7 38.8 %copy-start.2 = (bf16[2,2,64,512]{3,2,1,0:T(8,128)(2,1)}, bf16[2,2,64,512]{3,2,1,0:T(8,128)(2,1)S(1)}, u32[]{:S(2)}) copy-start(bf16[2,2,64,512]{3,2,1,0:T(8,128)(2,1)S(1)} %collective-permute-done.4) | copy-start | bytes 786436
  142.8 2.4 slice-start
  142.8 2.4 copy-start.10
  145.2 5.2 %copy-start.1 = (f32[2,2,64,256,4]{3,2,4,1,0:T(8,128)S(1)}, f32[2,2,64,256,4]{3,2,4,1,0:T(8,128)}, u32[]{:S(2)}) copy-start(f32[2,2,64,256,4]{3,2,4,1,0:T(8,128)} %get-tuple-element.643) | copy-start | bytes 3145732 | tf_op jit(solution)/shard_map/while
  158.4 60.2 %collective-permute-start.6 = (bf16[2,2,4,256,256]{4,3,2,1,0:T(8,128)(2,1)}, bf16[2,2,4,256,256]{4,3,2,1,0:T(8,128)(2,1)}, u32[]{:S(2)}, u32[]{:S(2)}) collective-permute-start(bf16[2,2,4,256,256]{4,3,2,1,0:T(8,128)(2,1)} %convert_element_type.124), channel_id=1, source_target_pairs={{0,128},{128,0},{4,132},{132,4},{8,136},{136,8},{12,140},{140,12},... | collective-permute-start | bytes 6291464 | tf_op jit(solution)/shard_map/ppermute | solution.py:27
  158.7 2.4 copy-start.9
  161.1 6.9 %copy-start.5 = (pred[2,256,68]{1,2,0:T(8,128)(4,1)S(1)}, pred[2,256,68]{1,2,0:T(8,128)(4,1)}, u32[]{:S(2)}) copy-start(pred[2,256,68]{1,2,0:T(8,128)(4,1)} %fusion.81) | copy-start | bytes 104452
  168.0 2.2 copy-start.6
  173.1 25.4 %collective-permute-start.7 = (bf16[2,2,4,256]{3,2,1,0:T(4,128)(2,1)S(1)}, bf16[2,2,4,256]{3,2,1,0:T(4,128)(2,1)S(1)}, u32[]{:S(2)}, u32[]{:S(2)}) collective-permute-start(bf16[2,2,4,256]{3,2,1,0:T(4,128)(2,1)S(1)} %convert_element_type.128), channel_id=1, source_target_pairs={{0,128},{128,0},{4,132},{132,4},{8,136},{136,8},{12,140},{140,12},... | collective-permute-start | bytes 24584 | tf_op jit(solution)/shard_map/ppermute | solution.py:27
  174.3 24.2 %collective-permute-start.5 = (bf16[2,2,4,256]{3,2,1,0:T(4,128)(2,1)S(1)}, bf16[2,2,4,256]{3,2,1,0:T(4,128)(2,1)S(1)}, u32[]{:S(2)}, u32[]{:S(2)}) collective-permute-start(bf16[2,2,4,256]{3,2,1,0:T(4,128)(2,1)S(1)} %convert_element_type.119), channel_id=1, source_target_pairs={{0,128},{128,0},{4,132},{132,4},{8,136},{136,8},{12,140},{140,12},... | collective-permute-start | bytes 24584 | tf_op jit(solution)/shard_map/ppermute | solution.py:27
  199.2 15.5 %all-to-all-start.2 = ((bf16[1,2,8,256]{3,1,0,2:T(2,128)(2,1)}), bf16[1,2,8,256]{3,1,0,2:T(2,128)(2,1)S(1)}, u32[]{:S(2)}, u32[]{:S(2)}) async-start(bf16[1,2,8,256]{3,1,0,2:T(2,128)(2,1)} %bitcast.34), calls=%async_computation.2 | async-start | bytes 16384 | tf_op jit(solution)/shard_map/all_to_all | solution.py:267
  214.6 11.3 %all-to-all-start = ((bf16[1,2,8,256]{3,1,0,2:T(2,128)(2,1)}), bf16[1,2,8,256]{3,1,0,2:T(2,128)(2,1)S(1)}, u32[]{:S(2)}, u32[]{:S(2)}) async-start(bf16[1,2,8,256]{3,1,0,2:T(2,128)(2,1)} %bitcast.21), calls=%async_computation | async-start | bytes 16384 | tf_op jit(solution)/shard_map/all_to_all | solution.py:266
  226.0 31.1 %all-to-all-start.1 = ((bf16[1,2,8,256,256]{4,3,1,0,2:T(8,128)(2,1)}), bf16[1,2,8,256,256]{4,3,1,0,2:T(8,128)(2,1)}, u32[]{:S(2)}, u32[]{:S(2)}) async-start(bf16[1,2,8,256,256]{4,3,1,0,2:T(8,128)(2,1)} %copy.41), calls=%async_computation.1 | async-start | bytes 4194304 | tf_op jit(solution)/shard_map/all_to_all | solution.py:268
  230.8 74.7 %reduce-scatter.2.cloned.1.call-start = ((), (), s32[]{:S(2)}) async-start(), calls=%async_computation.7 | async-start | bytes 2621440 | tf_op jit(solution)/shard_map/reduce_scatter | solution.py:280
  262.2 51.8 %copy-start.3 = (bf16[2,256,512]{2,1,0:T(8,128)(2,1)S(1)}, bf16[2,256,512]{2,1,0:T(8,128)(2,1)}, u32[]{:S(2)}) copy-start(bf16[2,256,512]{2,1,0:T(8,128)(2,1)} %param.16) | copy-start | bytes 1572868
  262.2 51.8 %copy-start.8 = (f32[512]{0:T(512)S(1)}, f32[512]{0:T(512)}, u32[]{:S(2)}) copy-start(f32[512]{0:T(512)} %param.21) | copy-start | bytes 6148
Sparse Core Ops, SparseCore 0:
  9.2 33.3 all-gather.3
  53.9 28.5 all-gather.5
  88.8 29.6 all-gather.7
  262.4 43.0 reduce-scatter.1
where the time goes:
time: 324 us; the launch traced here: 323 us
  waiting for transfers between devices  183 us (56%)
  other arithmetic  41.6 us (13%)
  matrix products  27.9 us (9%)
  starting transfers between devices  24.8 us (8%)
  local copies, waits for them, and re-layouts  19.1 us (6%)
  between operations  18.6 us (6%)
  blocking collectives  7.38 us (2%)
    reduce_scatter x1, waiting for transfers between devices, per_device(): lax.psum_scatter(terms.astype(jnp.bfloat16), 'tp', scatter_dimension=2, t...  43.2 us
    ppermute x8, waiting for transfers between devices, partner(): return lax.ppermute(block, axis, route)  39.7 us
    all_gather x1, waiting for transfers between devices, per_device(): gathered = lax.all_gather(hidden_in, 'tp', axis=2, tiled=True)  32.2 us
    all_to_all x1, waiting for transfers between devices, per_device(): lax.all_to_all(as_sent(weighted[None]), 'tp', split_axis=2, concat_axis=0...  26.3 us
    all_gather x1, waiting for transfers between devices, per_device(): lax.all_gather(query_part, 'tp', axis=2, tiled=True)  19.1 us
    all_gather x1, waiting for transfers between devices, per_device(): lax.all_gather(pair_part, 'tp', axis=2, tiled=True)  17.8 us
    dot_general x3, matrix products, step(): jnp.einsum('rvgcb,rvbd->rvgcd', weights.astype(jnp.bfloat16), values, pre...  11 us
    all_to_all x1, starting transfers between devices, per_device(): lax.all_to_all(as_sent(row_total[None]), 'tp', split_axis=2, concat_axis=...  10.9 us
  transfers between devices with their start and end apart: 15, of which 9 were waited for; matrix products, arithmetic and copies ran while one was open for 16% of the time, Pallas kernels for 0%

commit v1 on v0

v1 whole, which is shorter than its diff:
```python
import math

import jax
import jax.numpy as jnp
from jax import lax
from jax.experimental import pallas as pl
from jax.experimental.pallas import tpu as pltpu
from jax.sharding import PartitionSpec as P

D = 2048
HEADS = 8
KVH = 2
HD = 256
WIN = 512
SINK = 4
SPAN = 256
EPS = 1e-06
NEG = -1e30

REQ = 2
TP = 4
FEAT = D // TP
SLOTS = WIN // TP
HALF = SPAN // 2
COLS = WIN + SPAN + 128
MESH = pl.DeviceIdType.MESH
F32 = jnp.float32
BF16 = jnp.bfloat16


def layer_kernel(
    cached_ref,
    span_ref,
    sinkn_ref,
    reach_ref,
    hid,
    ng,
    qw,
    kvw,
    ow,
    pg,
    sink,
    win,
    out,
    xg,
    wq,
    wkv,
    wo,
    gain,
    pgain,
    sinkb,
    kvb,
    qb,
    biasb,
    cosb,
    sinb,
    attb,
    ownb,
    sendb,
    recvb,
    ssb,
    outb,
    lsem,
    osem,
    ssem,
    rsem,
):
    r = lax.axis_index("req")
    t = lax.axis_index("tp")
    core = lax.rem(t, 2)
    chip = lax.div(t, 2)
    other = 1 - chip
    tc = 2 * chip + 1 - core
    to = 2 * other + core
    tx = 2 * other + 1 - core

    def columns(i):
        return pl.ds(pl.multiple_of(i * FEAT, FEAT), FEAT)

    def slots(i):
        return pl.ds(pl.multiple_of(i * SLOTS, SLOTS), SLOTS)

    local = {}

    def fetch(name, src, dst):
        copy = pltpu.make_async_copy(src, dst, lsem.at[len(local)])
        copy.start()
        local[name] = copy

    remote = {}

    def make(name, src, dst, target):
        i = len(remote)
        remote[name] = pltpu.make_async_remote_copy(
            src_ref=src,
            dst_ref=dst,
            send_sem=ssem.at[i],
            recv_sem=rsem.at[i],
            device_id=(r, target),
            device_id_type=MESH,
        )
        return remote[name]

    fetch("gain", ng, gain)
    for q in range(REQ):
        fetch(("hid", q), hid.at[q], xg.at[q, t])
    fetch("wq", qw, wq)
    fetch("wkv", kvw, wkv)
    for q in range(REQ):
        for k in range(2):
            fetch(
                ("win", q, k),
                win.at[q, chip, :, k * HD : (k + 1) * HD],
                kvb.at[k, q, slots(t)],
            )
    fetch("sink", sink.at[:, chip], sinkb)
    fetch("wo0", ow.at[:, columns(t)], wo.at[core, 0])
    fetch("wo1", ow.at[:, columns(to)], wo.at[core, 1])
    fetch("pg", pg, pgain)

    barrier = pltpu.get_barrier_semaphore()
    for peer in (tc, to, tx):
        pl.semaphore_signal(barrier, inc=1, device_id=(r, peer), device_id_type=MESH)
    pl.semaphore_wait(barrier, 3)

    pieces = [(q, h) for q in range(REQ) for h in range(2)]
    for q in range(REQ):
        for h in range(2):
            rows = pl.ds(h * HALF, HALF)
            make(("H", q, h), hid.at[q, rows], xg.at[q, t, rows], to).start()
        make(("D", q), hid.at[q], xg.at[q, t], tc).start()
        for k in range(2):
            lanes = slice(k * HD, (k + 1) * HD)
            make(("C", q, k), win.at[q, other, :, lanes], kvb.at[k, q, slots(t)], to).start()
    for q in range(REQ):
        for k in range(2):
            lanes = slice(k * HD, (k + 1) * HD)
            make(("E", q, k), win.at[q, chip, :, lanes], kvb.at[k, q, slots(t)], tc).start()
    make(("W", 0), ow.at[:, columns(tc)], wo.at[core, 0], tc).start()
    make(("W", 1), ow.at[:, columns(tx)], wo.at[core, 1], tc).start()
    for q, h in pieces:
        rows = pl.ds(h * HALF, HALF)
        make(("HF", q, h), xg.at[q, to, rows], xg.at[q, to, rows], tc)
        new_rows = pl.ds(WIN + h * HALF, HALF)
        make(("N", q, h), kvb.at[core, q, new_rows], kvb.at[core, q, new_rows], tc)
        make(("A", q, h), attb.at[q, core, rows], attb.at[q, core, rows], tc)
        make(("O", q, h), sendb.at[q, h], recvb.at[q, h], to)
        for name, peer in (("c", tc), ("o", to), ("x", tx)):
            make(("S" + name, q, h), ssb.at[q, h, t], ssb.at[q, h, t], peer)
    for q in range(REQ):
        for k in range(2):
            make(("CF", q, k), kvb.at[k, q, slots(to)], kvb.at[k, q, slots(to)], tc)

    lane = lax.broadcasted_iota(jnp.int32, (HALF, HD // 2), 1).astype(F32)
    frequency = jnp.exp(lane * (-2.0 * math.log(10000.0) / HD))
    for q, h in pieces:
        row = lax.broadcasted_iota(jnp.int32, (HALF, HD // 2), 0) + h * HALF
        angles = (row + cached_ref[q]).astype(F32) * frequency
        cosb[q, h] = jnp.cos(angles)
        sinb[q, h] = jnp.sin(angles)
    for q, h in pieces:
        cached, fresh, sinks, reach = cached_ref[q], span_ref[q], sinkn_ref[q], reach_ref[q]
        row = lax.broadcasted_iota(jnp.int32, (HALF, WIN), 0) + h * HALF
        col = lax.broadcasted_iota(jnp.int32, (HALF, WIN), 1)
        allowed = (col >= sinks + WIN - cached) & (row + WIN - col < reach)
        biasb[q, h, :, 0:WIN] = jnp.where(allowed, 0.0, NEG)
        row = lax.broadcasted_iota(jnp.int32, (HALF, SPAN), 0) + h * HALF
        col = lax.broadcasted_iota(jnp.int32, (HALF, SPAN), 1)
        allowed = (col <= row) & (col < fresh) & (row - col < reach)
        biasb[q, h, :, WIN : WIN + SPAN] = jnp.where(allowed, 0.0, NEG)
        col = lax.broadcasted_iota(jnp.int32, (HALF, 128), 1)
        biasb[q, h, :, WIN + SPAN : COLS] = jnp.where(col < sinks, 0.0, NEG)
    local["sink"].wait()
    for q in range(REQ):
        for k in range(2):
            kvb[k, q, WIN + SPAN : COLS, :] = jnp.zeros((COLS - WIN - SPAN, HD), BF16)
            kvb[k, q, WIN + SPAN : WIN + SPAN + SINK, :] = sinkb[q, :, k * HD : (k + 1) * HD]
    local["gain"].wait()
    local["wq"].wait()
    local["wkv"].wait()

    def pass_on(q, h):
        remote["H", q, h].wait_recv()
        remote["HF", q, h].start()

    def pass_cache(q):
        for k in range(2):
            remote["C", q, k].wait_recv()
            remote["CF", q, k].start()

    def project(q, h):
        rows = slice(h * HALF, (h + 1) * HALF)
        if h == 0:
            local["hid", q].wait()
            remote["D", q].wait_recv()
        remote["HF", q, h].wait_recv()
        square = jnp.zeros((HALF, 1), F32)
        acc_q = jnp.zeros((HALF, 2 * HD), F32)
        acc_kv = jnp.zeros((HALF, HD), F32)
        for s in range(TP):
            span = slice(s * FEAT, (s + 1) * FEAT)
            x = xg[q, s, rows, :].astype(F32)
            square += jnp.sum(x * x, axis=-1, keepdims=True)
            scaled = (x * gain[:, span]).astype(BF16)
            acc_q += jnp.dot(scaled, wq[span, :], preferred_element_type=F32)
            acc_kv += jnp.dot(scaled, wkv[span, :], preferred_element_type=F32)
        scale = lax.rsqrt(square * (1.0 / D) + EPS)
        cosine, sine = cosb[q, h], sinb[q, h]
        cosine, sine = cosine * scale, sine * scale
        u, w = acc_kv[:, : HD // 2], acc_kv[:, HD // 2 :]
        is_key = core == 0
        cos_kv = jnp.where(is_key, cosine, jnp.broadcast_to(scale, cosine.shape))
        sin_kv = jnp.where(is_key, sine, 0.0)
        new_rows = slice(WIN + h * HALF, WIN + (h + 1) * HALF)
        kvb[core, q, new_rows, : HD // 2] = (u * cos_kv - w * sin_kv).astype(BF16)
        kvb[core, q, new_rows, HD // 2 :] = (w * cos_kv + u * sin_kv).astype(BF16)
        remote["N", q, h].start()
        cosine, sine = cosine * (1.0 / math.sqrt(HD)), sine * (1.0 / math.sqrt(HD))
        for n in range(2):
            u = acc_q[:, n * HD : n * HD + HD // 2]
            w = acc_q[:, n * HD + HD // 2 : (n + 1) * HD]
            qb[q, h, n, :, : HD // 2] = (u * cosine - w * sine).astype(BF16)
            qb[q, h, n, :, HD // 2 :] = (w * cosine + u * sine).astype(BF16)

    def keys_ready(q):
        for k in range(2):
            local["win", q, k].wait()
            remote["E", q, k].wait_recv()
            remote["CF", q, k].wait_recv()
        for h in range(2):
            remote["N", q, h].wait_recv()

    def attend(q, h):
        query = qb[q, h].reshape(2 * HALF, HD)
        scores = lax.dot_general(
            query, kvb[0, q], (((1,), (1,)), ((), ())), preferred_element_type=F32
        )
        scores = scores.reshape(2, HALF, COLS) + biasb[q, h][None]
        peak = jnp.max(scores, axis=-1, keepdims=True)
        weights = jnp.exp(scores - peak)
        total = jnp.sum(weights, axis=-1, keepdims=True).reshape(2 * HALF, 1)
        weights = weights.astype(BF16).reshape(2 * HALF, COLS)
        mixed = jnp.dot(weights, kvb[1, q], preferred_element_type=F32) * (1.0 / total)
        mixed = mixed.astype(BF16)
        rows = slice(h * HALF, (h + 1) * HALF)
        for n in range(2):
            attb[q, core, rows, n * HD : (n + 1) * HD] = mixed[n * HALF : (n + 1) * HALF]
        remote["A", q, h].start()

    def emit(q, h):
        rows = slice(h * HALF, (h + 1) * HALF)
        remote["A", q, h].wait_recv()
        first, second = attb[q, 0, rows, :], attb[q, 1, rows, :]
        lent = jnp.dot(first, wo[0, 1], preferred_element_type=F32) + jnp.dot(
            second, wo[1, 1], preferred_element_type=F32
        )
        sendb[q, h] = lent.astype(BF16)
        remote["O", q, h].start()
        ownb[q, h] = jnp.dot(first, wo[0, 0], preferred_element_type=F32) + jnp.dot(
            second, wo[1, 0], preferred_element_type=F32
        )

    def squares(q, h):
        remote["O", q, h].wait_recv()
        projected = ownb[q, h] + recvb[q, h].astype(F32)
        ownb[q, h] = projected
        square = jnp.sum(projected * projected, axis=-1, keepdims=True)
        turned = jnp.transpose(jnp.broadcast_to(square, (HALF, 128)))
        ssb[q, h, t] = turned[0:8, :]
        for name in ("Sc", "So", "Sx"):
            remote[name, q, h].start()

    stores = []

    def finish(q, h):
        for name in ("Sc", "So", "Sx"):
            remote[name, q, h].wait_recv()
        square = ssb[q, h, 0] + ssb[q, h, 1] + ssb[q, h, 2] + ssb[q, h, 3]
        scale = lax.rsqrt(square * (1.0 / D) + EPS)
        scale = jnp.transpose(jnp.broadcast_to(scale[0:1, :], (128, HALF)))[:, 0:1]
        rows = slice(h * HALF, (h + 1) * HALF)
        kept = xg[q, t, rows, :].astype(F32)
        outb[q, rows, :] = (kept + pgain[...] * ownb[q, h] * scale).astype(BF16)
        copy = pltpu.make_async_copy(
            outb.at[q, pl.ds(h * HALF, HALF)],
            out.at[q, pl.ds(h * HALF, HALF)],
            osem.at[2 * q + h],
        )
        copy.start()
        stores.append(copy)

    pass_on(0, 0)
    project(0, 0)
    pass_on(0, 1)
    project(0, 1)
    pass_cache(0)
    keys_ready(0)
    attend(0, 0)
    attend(0, 1)
    pass_on(1, 0)
    for name in ("wo0", "wo1", "pg"):
        local[name].wait()
    for i in range(2):
        remote["W", i].wait_recv()
    emit(0, 0)
    emit(0, 1)
    pass_on(1, 1)
    project(1, 0)
    project(1, 1)
    pass_cache(1)
    keys_ready(1)
    attend(1, 0)
    attend(1, 1)
    emit(1, 0)
    emit(1, 1)
    squares(0, 0)
    squares(0, 1)
    finish(0, 0)
    finish(0, 1)
    squares(1, 0)
    squares(1, 1)
    finish(1, 0)
    finish(1, 1)
    for copy in remote.values():
        copy.wait_send()
    for copy in stores:
        copy.wait()


def per_device(
    hidden_in,
    norm_gain,
    q_weight,
    kv_weight,
    out_weight,
    post_gain,
    sink_cache,
    window_cache,
    cached_len,
    span_len,
    sink_count,
    window_size,
):
    anywhere = pl.BlockSpec(memory_space=pl.ANY)
    scalars = pl.BlockSpec(memory_space=pltpu.SMEM)
    copies = 52
    return pl.pallas_call(
        layer_kernel,
        out_shape=jax.ShapeDtypeStruct((REQ, SPAN, FEAT), BF16),
        in_specs=[scalars] * 4 + [anywhere] * 8,
        out_specs=anywhere,
        scratch_shapes=[
            pltpu.VMEM((REQ, TP, SPAN, FEAT), BF16),
            pltpu.VMEM((D, 2 * HD), BF16),
            pltpu.VMEM((D, HD), BF16),
            pltpu.VMEM((2, 2, 2 * HD, FEAT), BF16),
            pltpu.VMEM((1, D), F32),
            pltpu.VMEM((1, FEAT), F32),
            pltpu.VMEM((REQ, SINK, 2 * HD), BF16),
            pltpu.VMEM((2, REQ, COLS, HD), BF16),
            pltpu.VMEM((REQ, 2, 2, HALF, HD), BF16),
            pltpu.VMEM((REQ, 2, HALF, COLS), F32),
            pltpu.VMEM((REQ, 2, HALF, HD // 2), F32),
            pltpu.VMEM((REQ, 2, HALF, HD // 2), F32),
            pltpu.VMEM((REQ, 2, SPAN, 2 * HD), BF16),
            pltpu.VMEM((REQ, 2, HALF, FEAT), F32),
            pltpu.VMEM((REQ, 2, HALF, FEAT), BF16),
            pltpu.VMEM((REQ, 2, HALF, FEAT), BF16),
            pltpu.VMEM((REQ, 2, TP, 8, HALF), F32),
            pltpu.VMEM((REQ, SPAN, FEAT), BF16),
            pltpu.SemaphoreType.DMA((16,)),
            pltpu.SemaphoreType.DMA((4,)),
            pltpu.SemaphoreType.DMA((copies,)),
            pltpu.SemaphoreType.DMA((copies,)),
        ],
        compiler_params=pltpu.CompilerParams(
            collective_id=0, has_side_effects=True, vmem_limit_bytes=60 * 2**20
        ),
    )(
        cached_len,
        span_len,
        sink_count,
        window_size,
        hidden_in,
        norm_gain.reshape(1, D),
        q_weight,
        kv_weight,
        out_weight,
        post_gain.reshape(1, FEAT),
        sink_cache,
        window_cache,
    )


def solution(mesh):
    in_specs = (
        P("req", None, "tp"),
        P(),
        P(None, "tp"),
        P(None, "tp"),
        P("tp", None),
        P("tp"),
        P("req", None, None, None),
        P("req", None, "tp", None),
        P("req"),
        P("req"),
        P("req"),
        P("req"),
    )
    return jax.shard_map(
        per_device,
        mesh=mesh,
        in_specs=in_specs,
        out_specs=P("req", None, "tp"),
        check_vma=False,
    )
```

time: 324 us -> 45.5 us (0.14)
  waiting for transfers between devices: 183 us -> 0 us
  Pallas kernels: 0 us -> 43.5 us
  other arithmetic: 41.6 us -> 0 us
  matrix products: 27.9 us -> 0 us
  starting transfers between devices: 24.8 us -> 0 us
  between operations: 18.6 us -> 0.01 us
  local copies, waits for them, and re-layouts: 19.1 us -> 1.87 us
  blocking collectives: 7.38 us -> 0 us
    all_gather x3 -> x0, waiting for transfers between devices: 69.1 us -> none  [the longest x1 32.2 us: per_device(): gathered = lax.all_gather(hidden_in, 'tp', axis=2, tiled=True)]
    pallas_call x0 -> x1, Pallas kernels: none -> 43.5 us  [per_device(): pl.pallas_call(layer_kernel, out_shape=jax.ShapeDtypeStruct((REQ, SPAN, F...]
    reduce_scatter x1 -> x0, waiting for transfers between devices: 43.2 us -> none  [per_device(): lax.psum_scatter(terms.astype(jnp.bfloat16), 'tp', scatter_dimension=2, t...]
    ppermute x8 -> x0, waiting for transfers between devices: 39.7 us -> none  [partner(): return lax.ppermute(block, axis, route)]
    all_to_all x3 -> x0, waiting for transfers between devices: 30.2 us -> none  [the longest x1 26.3 us: per_device(): lax.all_to_all(as_sent(weighted[None]), 'tp', split_axis=2, concat_axis=0...]
    dot_general x9 -> x0, matrix products: 27.9 us -> none  [the longest x3 11 us: step(): jnp.einsum('rvgcb,rvbd->rvgcd', weights.astype(jnp.bfloat16), values, pre...]
    all_to_all x3 -> x0, starting transfers between devices: 19.6 us -> none  [the longest x1 10.9 us: per_device(): lax.all_to_all(as_sent(row_total[None]), 'tp', split_axis=2, concat_axis=...]
    convert_element_type x8 -> x0, other arithmetic: 13.5 us -> none  [the longest x3 5.97 us: as_sent(): a.astype(jnp.bfloat16)]
  transfers between devices with their start and end apart: 15 -> 0, of which waited for: 9 -> 0; matrix products, arithmetic and copies ran while one was open for 16% -> 0% of each run, Pallas kernels for 0% -> 0%
where the time goes in v1:
time: 45.5 us; the launch traced here: 45.4 us
  Pallas kernels  43.5 us (96%)
  local copies, waits for them, and re-layouts  1.87 us (4%)
    pallas_call x1, Pallas kernels, per_device(): pl.pallas_call(layer_kernel, out_shape=jax.ShapeDtypeStruct((REQ, SPAN, F...  43.5 us
    unnamed x1, local copies, waits for them, and re-layouts  1.87 us

profile of v1, /device:TPU:1, one launch (start us, length us, event | category | flops | bytes accessed | tf_op | source)
XLA Modules:
  0.0 45.4 jit_solution(3559224657006600334)
XLA Ops:
  0.0 43.5 %shard_map.118 = bf16[2,256,512]{2,1,0:T(8,128)(2,1)} custom-call(s32[2]{0:T(128)} %cached_ref.1, s32[2]{0:T(128)} %span_ref.1, s32[2]{0:T(128)} %sinkn_ref.1, s32[2]{0:T(128)} %reach_ref.1, bf16[2,256,512]{2,1,0:T(8,128)(2,1)} %hid.1, f32[1,2048]{1,0:T(1,128)} %bitcast.2, bf16[2048,512]{1,0:T(8,128)(2,1)} %qw.1, bf16[2048,256]{1,0:T(8,128)(2,1)} %kvw.1, ...), custom_call_target="tpu_custom_call" | custom-call | tf_op jit(solution)/shard_map/pallas_call | solution.py:347
  43.5 1.9 %copy.14 = bf16[2,256,512]{2,1,0:T(8,128)(2,1)} copy(bf16[2,256,512]{2,1,0:T(8,128)(2,1)} %shard_map.118) | data formatting | bytes 1048576

commit v2 on v1

--- a/solution.py
+++ b/solution.py
@@ -22,17 +22,22 @@
 FEAT = D // TP
 SLOTS = WIN // TP
 HALF = SPAN // 2
-COLS = WIN + SPAN + 128
+PAD = 128
+NEW = PAD + WIN
+COLS = NEW + SPAN
+OUTS = ((0, 0, 0, HALF), (0, 1, 0, HALF), (1, 0, 0, HALF)) + tuple(
+    (1, 1, i * 32, 32) for i in range(4)
+)
 MESH = pl.DeviceIdType.MESH
 F32 = jnp.float32
 BF16 = jnp.bfloat16
 
 
 def layer_kernel(
-    cached_ref,
-    span_ref,
-    sinkn_ref,
-    reach_ref,
+    cached_in,
+    span_in,
+    sinkn_in,
+    reach_in,
     hid,
     ng,
     qw,
@@ -42,6 +47,10 @@
     sink,
     win,
     out,
+    cached_ref,
+    span_ref,
+    sinkn_ref,
+    reach_ref,
     xg,
     wq,
     wkv,
@@ -74,11 +83,15 @@
     to = 2 * other + core
     tx = 2 * other + 1 - core
 
+    barrier = pltpu.get_barrier_semaphore()
+    for peer in (to, tx, tc):
+        pl.semaphore_signal(barrier, inc=1, device_id=(r, peer), device_id_type=MESH)
+
     def columns(i):
         return pl.ds(pl.multiple_of(i * FEAT, FEAT), FEAT)
 
     def slots(i):
-        return pl.ds(pl.multiple_of(i * SLOTS, SLOTS), SLOTS)
+        return pl.ds(pl.multiple_of(PAD + i * SLOTS, SLOTS), SLOTS)
 
     local = {}
 
@@ -101,6 +114,10 @@
         )
         return remote[name]
 
+    fetch("cached", cached_in, cached_ref)
+    fetch("span", span_in, span_ref)
+    fetch("sinkn", sinkn_in, sinkn_ref)
+    fetch("reach", reach_in, reach_ref)
     fetch("gain", ng, gain)
     for q in range(REQ):
         fetch(("hid", q), hid.at[q], xg.at[q, t])
@@ -118,20 +135,27 @@
     fetch("wo1", ow.at[:, columns(to)], wo.at[core, 1])
     fetch("pg", pg, pgain)
 
-    barrier = pltpu.get_barrier_semaphore()
-    for peer in (tc, to, tx):
-        pl.semaphore_signal(barrier, inc=1, device_id=(r, peer), device_id_type=MESH)
     pl.semaphore_wait(barrier, 3)
 
     pieces = [(q, h) for q in range(REQ) for h in range(2)]
-    for q in range(REQ):
-        for h in range(2):
-            rows = pl.ds(h * HALF, HALF)
-            make(("H", q, h), hid.at[q, rows], xg.at[q, t, rows], to).start()
-        make(("D", q), hid.at[q], xg.at[q, t], tc).start()
+
+    def send_rows(q, h):
+        rows = pl.ds(h * HALF, HALF)
+        make(("H", q, h), hid.at[q, rows], xg.at[q, t, rows], to).start()
+
+    def send_cache(q):
         for k in range(2):
             lanes = slice(k * HD, (k + 1) * HD)
             make(("C", q, k), win.at[q, other, :, lanes], kvb.at[k, q, slots(t)], to).start()
+
+    send_rows(0, 0)
+    send_rows(0, 1)
+    send_cache(0)
+    send_rows(1, 0)
+    send_cache(1)
+    send_rows(1, 1)
+    for q in range(REQ):
+        make(("D", q), hid.at[q], xg.at[q, t], tc).start()
     for q in range(REQ):
         for k in range(2):
             lanes = slice(k * HD, (k + 1) * HD)
@@ -141,16 +165,20 @@
     for q, h in pieces:
         rows = pl.ds(h * HALF, HALF)
         make(("HF", q, h), xg.at[q, to, rows], xg.at[q, to, rows], tc)
-        new_rows = pl.ds(WIN + h * HALF, HALF)
+        new_rows = pl.ds(NEW + h * HALF, HALF)
         make(("N", q, h), kvb.at[core, q, new_rows], kvb.at[core, q, new_rows], tc)
         make(("A", q, h), attb.at[q, core, rows], attb.at[q, core, rows], tc)
-        make(("O", q, h), sendb.at[q, h], recvb.at[q, h], to)
-        for name, peer in (("c", tc), ("o", to), ("x", tx)):
-            make(("S" + name, q, h), ssb.at[q, h, t], ssb.at[q, h, t], peer)
+    for i, (q, h, first, count) in enumerate(OUTS):
+        rows = pl.ds(first, count)
+        make(("O", i), sendb.at[q, h, rows], recvb.at[q, h, rows], to)
+        for name, peer in (("o", to), ("x", tx), ("c", tc)):
+            make(("S" + name, i), ssb.at[i, t], ssb.at[i, t], peer)
     for q in range(REQ):
         for k in range(2):
             make(("CF", q, k), kvb.at[k, q, slots(to)], kvb.at[k, q, slots(to)], tc)
 
+    for name in ("cached", "span", "sinkn", "reach"):
+        local[name].wait()
     lane = lax.broadcasted_iota(jnp.int32, (HALF, HD // 2), 1).astype(F32)
     frequency = jnp.exp(lane * (-2.0 * math.log(10000.0) / HD))
     for q, h in pieces:
@@ -163,18 +191,18 @@
         row = lax.broadcasted_iota(jnp.int32, (HALF, WIN), 0) + h * HALF
         col = lax.broadcasted_iota(jnp.int32, (HALF, WIN), 1)
         allowed = (col >= sinks + WIN - cached) & (row + WIN - col < reach)
-        biasb[q, h, :, 0:WIN] = jnp.where(allowed, 0.0, NEG)
+        biasb[q, h, :, PAD:NEW] = jnp.where(allowed, 0.0, NEG)
         row = lax.broadcasted_iota(jnp.int32, (HALF, SPAN), 0) + h * HALF
         col = lax.broadcasted_iota(jnp.int32, (HALF, SPAN), 1)
         allowed = (col <= row) & (col < fresh) & (row - col < reach)
-        biasb[q, h, :, WIN : WIN + SPAN] = jnp.where(allowed, 0.0, NEG)
-        col = lax.broadcasted_iota(jnp.int32, (HALF, 128), 1)
-        biasb[q, h, :, WIN + SPAN : COLS] = jnp.where(col < sinks, 0.0, NEG)
+        biasb[q, h, :, NEW:COLS] = jnp.where(allowed, 0.0, NEG)
+        col = lax.broadcasted_iota(jnp.int32, (HALF, PAD), 1)
+        biasb[q, h, :, 0:PAD] = jnp.where(col < jnp.minimum(sinks, SINK), 0.0, NEG)
     local["sink"].wait()
     for q in range(REQ):
         for k in range(2):
-            kvb[k, q, WIN + SPAN : COLS, :] = jnp.zeros((COLS - WIN - SPAN, HD), BF16)
-            kvb[k, q, WIN + SPAN : WIN + SPAN + SINK, :] = sinkb[q, :, k * HD : (k + 1) * HD]
+            kvb[k, q, 0:PAD, :] = jnp.zeros((PAD, HD), BF16)
+            kvb[k, q, 0:SINK, :] = sinkb[q, :, k * HD : (k + 1) * HD]
     local["gain"].wait()
     local["wq"].wait()
     local["wkv"].wait()
@@ -211,7 +239,7 @@
         is_key = core == 0
         cos_kv = jnp.where(is_key, cosine, jnp.broadcast_to(scale, cosine.shape))
         sin_kv = jnp.where(is_key, sine, 0.0)
-        new_rows = slice(WIN + h * HALF, WIN + (h + 1) * HALF)
+        new_rows = slice(NEW + h * HALF, NEW + (h + 1) * HALF)
         kvb[core, q, new_rows, : HD // 2] = (u * cos_kv - w * sin_kv).astype(BF16)
         kvb[core, q, new_rows, HD // 2 :] = (w * cos_kv + u * sin_kv).astype(BF16)
         remote["N", q, h].start()
@@ -227,20 +255,20 @@
             local["win", q, k].wait()
             remote["E", q, k].wait_recv()
             remote["CF", q, k].wait_recv()
-        for h in range(2):
-            remote["N", q, h].wait_recv()
 
     def attend(q, h):
+        remote["N", q, h].wait_recv()
+        cols = NEW + (h + 1) * HALF
         query = qb[q, h].reshape(2 * HALF, HD)
         scores = lax.dot_general(
-            query, kvb[0, q], (((1,), (1,)), ((), ())), preferred_element_type=F32
+            query, kvb[0, q, :cols], (((1,), (1,)), ((), ())), preferred_element_type=F32
         )
-        scores = scores.reshape(2, HALF, COLS) + biasb[q, h][None]
+        scores = scores.reshape(2, HALF, cols) + biasb[q, h, :, :cols][None]
         peak = jnp.max(scores, axis=-1, keepdims=True)
         weights = jnp.exp(scores - peak)
         total = jnp.sum(weights, axis=-1, keepdims=True).reshape(2 * HALF, 1)
-        weights = weights.astype(BF16).reshape(2 * HALF, COLS)
-        mixed = jnp.dot(weights, kvb[1, q], preferred_element_type=F32) * (1.0 / total)
+        weights = weights.astype(BF16).reshape(2 * HALF, cols)
+        mixed = jnp.dot(weights, kvb[1, q, :cols], preferred_element_type=F32) * (1.0 / total)
         mixed = mixed.astype(BF16)
         rows = slice(h * HALF, (h + 1) * HALF)
         for n in range(2):
@@ -255,37 +283,44 @@
             second, wo[1, 1], preferred_element_type=F32
         )
         sendb[q, h] = lent.astype(BF16)
-        remote["O", q, h].start()
+        for i, piece in enumerate(OUTS):
+            if piece[:2] == (q, h):
+                remote["O", i].start()
         ownb[q, h] = jnp.dot(first, wo[0, 0], preferred_element_type=F32) + jnp.dot(
             second, wo[1, 0], preferred_element_type=F32
         )
 
-    def squares(q, h):
-        remote["O", q, h].wait_recv()
-        projected = ownb[q, h] + recvb[q, h].astype(F32)
-        ownb[q, h] = projected
+    def diagonal(count):
+        row = lax.broadcasted_iota(jnp.int32, (count, 128), 0)
+        return row == lax.broadcasted_iota(jnp.int32, (count, 128), 1)
+
+    def squares(i):
+        q, h, first, count = OUTS[i]
+        rows = slice(first, first + count)
+        remote["O", i].wait_recv()
+        projected = ownb[q, h, rows, :] + recvb[q, h, rows, :].astype(F32)
+        ownb[q, h, rows, :] = projected
         square = jnp.sum(projected * projected, axis=-1, keepdims=True)
-        turned = jnp.transpose(jnp.broadcast_to(square, (HALF, 128)))
-        ssb[q, h, t] = turned[0:8, :]
-        for name in ("Sc", "So", "Sx"):
-            remote[name, q, h].start()
+        turned = jnp.sum(jnp.where(diagonal(count), square, 0.0), axis=0, keepdims=True)
+        ssb[i, t] = jnp.broadcast_to(turned, (8, 128))
+        for name in ("So", "Sx", "Sc"):
+            remote[name, i].start()
 
     stores = []
 
-    def finish(q, h):
-        for name in ("Sc", "So", "Sx"):
-            remote[name, q, h].wait_recv()
-        square = ssb[q, h, 0] + ssb[q, h, 1] + ssb[q, h, 2] + ssb[q, h, 3]
-        scale = lax.rsqrt(square * (1.0 / D) + EPS)
-        scale = jnp.transpose(jnp.broadcast_to(scale[0:1, :], (128, HALF)))[:, 0:1]
-        rows = slice(h * HALF, (h + 1) * HALF)
+    def finish(i):
+        q, h, first, count = OUTS[i]
+        for name in ("So", "Sx", "Sc"):
+            remote[name, i].wait_recv()
+        square = ssb[i, 0] + ssb[i, 1] + ssb[i, 2] + ssb[i, 3]
+        scale = lax.rsqrt(square * (1.0 / D) + EPS)[0:1, :]
+        scale = jnp.sum(jnp.where(diagonal(count), scale, 0.0), axis=-1, keepdims=True)
+        rows = slice(h * HALF + first, h * HALF + first + count)
         kept = xg[q, t, rows, :].astype(F32)
-        outb[q, rows, :] = (kept + pgain[...] * ownb[q, h] * scale).astype(BF16)
-        copy = pltpu.make_async_copy(
-            outb.at[q, pl.ds(h * HALF, HALF)],
-            out.at[q, pl.ds(h * HALF, HALF)],
-            osem.at[2 * q + h],
-        )
+        projected = ownb[q, h, first : first + count, :]
+        outb[q, rows, :] = (kept + pgain[...] * projected * scale).astype(BF16)
+        span = pl.ds(h * HALF + first, count)
+        copy = pltpu.make_async_copy(outb.at[q, span], out.at[q, span], osem.at[i])
         copy.start()
         stores.append(copy)
 
@@ -304,23 +339,22 @@
         remote["W", i].wait_recv()
     emit(0, 0)
     emit(0, 1)
-    pass_on(1, 1)
     project(1, 0)
-    project(1, 1)
     pass_cache(1)
     keys_ready(1)
     attend(1, 0)
+    pass_on(1, 1)
+    emit(1, 0)
+    project(1, 1)
     attend(1, 1)
-    emit(1, 0)
     emit(1, 1)
-    squares(0, 0)
-    squares(0, 1)
-    finish(0, 0)
-    finish(0, 1)
-    squares(1, 0)
-    squares(1, 1)
-    finish(1, 0)
-    finish(1, 1)
+    for i in range(len(OUTS)):
+        squares(i)
+        if i == 2:
+            finish(0)
+            finish(1)
+    for i in range(2, len(OUTS)):
+        finish(i)
     for copy in remote.values():
         copy.wait_send()
     for copy in stores:
@@ -342,14 +376,17 @@
     window_size,
 ):
     anywhere = pl.BlockSpec(memory_space=pl.ANY)
-    scalars = pl.BlockSpec(memory_space=pltpu.SMEM)
-    copies = 52
+    copies = 70
     return pl.pallas_call(
         layer_kernel,
         out_shape=jax.ShapeDtypeStruct((REQ, SPAN, FEAT), BF16),
-        in_specs=[scalars] * 4 + [anywhere] * 8,
+        in_specs=[anywhere] * 12,
         out_specs=anywhere,
         scratch_shapes=[
+            pltpu.SMEM((REQ,), jnp.int32),
+            pltpu.SMEM((REQ,), jnp.int32),
+            pltpu.SMEM((REQ,), jnp.int32),
+            pltpu.SMEM((REQ,), jnp.int32),
             pltpu.VMEM((REQ, TP, SPAN, FEAT), BF16),
             pltpu.VMEM((D, 2 * HD), BF16),
             pltpu.VMEM((D, HD), BF16),
@@ -366,10 +403,10 @@
             pltpu.VMEM((REQ, 2, HALF, FEAT), F32),
             pltpu.VMEM((REQ, 2, HALF, FEAT), BF16),
             pltpu.VMEM((REQ, 2, HALF, FEAT), BF16),
-            pltpu.VMEM((REQ, 2, TP, 8, HALF), F32),
+            pltpu.VMEM((len(OUTS), TP, 8, 128), F32),
             pltpu.VMEM((REQ, SPAN, FEAT), BF16),
-            pltpu.SemaphoreType.DMA((16,)),
-            pltpu.SemaphoreType.DMA((4,)),
+            pltpu.SemaphoreType.DMA((20,)),
+            pltpu.SemaphoreType.DMA((len(OUTS),)),
             pltpu.SemaphoreType.DMA((copies,)),
             pltpu.SemaphoreType.DMA((copies,)),
         ],

time: 45.5 us -> 44.1 us (0.969)
  Pallas kernels: 43.5 us -> 42.1 us
    pallas_call x1, Pallas kernels: 43.5 us -> 42.1 us  [per_device(): pl.pallas_call(layer_kernel, out_shape=jax.ShapeDtypeStruct((REQ, SPAN, F...]
where the time goes in v2:
time: 44.1 us; the launch traced here: 44 us
  Pallas kernels  42.1 us (95%)
  local copies, waits for them, and re-layouts  1.87 us (4%)
    pallas_call x1, Pallas kernels, per_device(): pl.pallas_call(layer_kernel, out_shape=jax.ShapeDtypeStruct((REQ, SPAN, F...  42.1 us
    unnamed x1, local copies, waits for them, and re-layouts  1.87 us

profile of v2, /device:TPU:1, one launch (start us, length us, event | category | flops | bytes accessed | tf_op | source)
XLA Modules:
  0.0 44.0 jit_solution(16261684699590627436)
XLA Ops:
  0.0 42.1 %shard_map.118 = bf16[2,256,512]{2,1,0:T(8,128)(2,1)} custom-call(s32[2]{0:T(128)} %cached_in.1, s32[2]{0:T(128)} %span_in.1, s32[2]{0:T(128)} %sinkn_in.1, s32[2]{0:T(128)} %reach_in.1, bf16[2,256,512]{2,1,0:T(8,128)(2,1)} %hid.1, f32[1,2048]{1,0:T(1,128)} %bitcast.2, bf16[2048,512]{1,0:T(8,128)(2,1)} %qw.1, bf16[2048,256]{1,0:T(8,128)(2,1)} %kvw.1, ...), custom_call_target="tpu_custom_call" | custom-call | tf_op jit(solution)/shard_map/pallas_call | solution.py:380
  42.1 1.9 %copy.14 = bf16[2,256,512]{2,1,0:T(8,128)(2,1)} copy(bf16[2,256,512]{2,1,0:T(8,128)(2,1)} %shard_map.118) | data formatting | bytes 1048576

commit v3 on v2

--- a/solution.py
+++ b/solution.py
@@ -68,9 +68,7 @@
     sendb,
     recvb,
     ssb,
-    outb,
     lsem,
-    osem,
     ssem,
     rsem,
 ):
@@ -306,8 +304,6 @@
         for name in ("So", "Sx", "Sc"):
             remote[name, i].start()
 
-    stores = []
-
     def finish(i):
         q, h, first, count = OUTS[i]
         for name in ("So", "Sx", "Sc"):
@@ -318,11 +314,7 @@
         rows = slice(h * HALF + first, h * HALF + first + count)
         kept = xg[q, t, rows, :].astype(F32)
         projected = ownb[q, h, first : first + count, :]
-        outb[q, rows, :] = (kept + pgain[...] * projected * scale).astype(BF16)
-        span = pl.ds(h * HALF + first, count)
-        copy = pltpu.make_async_copy(outb.at[q, span], out.at[q, span], osem.at[i])
-        copy.start()
-        stores.append(copy)
+        out[q, rows, :] = (kept + pgain[...] * projected * scale).astype(BF16)
 
     pass_on(0, 0)
     project(0, 0)
@@ -357,8 +349,6 @@
         finish(i)
     for copy in remote.values():
         copy.wait_send()
-    for copy in stores:
-        copy.wait()
 
 
 def per_device(
@@ -379,9 +369,9 @@
     copies = 70
     return pl.pallas_call(
         layer_kernel,
-        out_shape=jax.ShapeDtypeStruct((REQ, SPAN, FEAT), BF16),
+        out_shape=pltpu.VMEM((REQ, SPAN, FEAT), BF16),
         in_specs=[anywhere] * 12,
-        out_specs=anywhere,
+        out_specs=pl.BlockSpec(memory_space=pltpu.VMEM),
         scratch_shapes=[
             pltpu.SMEM((REQ,), jnp.int32),
             pltpu.SMEM((REQ,), jnp.int32),
@@ -404,9 +394,7 @@
             pltpu.VMEM((REQ, 2, HALF, FEAT), BF16),
             pltpu.VMEM((REQ, 2, HALF, FEAT), BF16),
             pltpu.VMEM((len(OUTS), TP, 8, 128), F32),
-            pltpu.VMEM((REQ, SPAN, FEAT), BF16),
             pltpu.SemaphoreType.DMA((20,)),
-            pltpu.SemaphoreType.DMA((len(OUTS),)),
             pltpu.SemaphoreType.DMA((copies,)),
             pltpu.SemaphoreType.DMA((copies,)),
         ],

time: 44.1 us -> 42.4 us (0.961)
  local copies, waits for them, and re-layouts: 1.87 us -> 0.8 us
  Pallas kernels: 42.1 us -> 41.5 us
    unnamed x1, local copies, waits for them, and re-layouts: 1.87 us -> 0.8 us
    pallas_call x1, Pallas kernels: 42.1 us -> 41.5 us  [per_device(): pl.pallas_call(layer_kernel, out_shape=pltpu.VMEM((REQ, SPAN, FEAT), BF16...]
where the time goes in v3:
time: 42.4 us; the launch traced here: 42.3 us
  Pallas kernels  41.5 us (98%)
  local copies, waits for them, and re-layouts  0.8 us (2%)
    pallas_call x1, Pallas kernels, per_device(): pl.pallas_call(layer_kernel, out_shape=pltpu.VMEM((REQ, SPAN, FEAT), BF16...  41.5 us

profile of v3, /device:TPU:1, one launch (start us, length us, event | category | flops | bytes accessed | tf_op | source)
XLA Modules:
  0.0 42.3 jit_solution(15875500170671370145)
XLA Ops:
  0.0 41.5 %shard_map.118 = bf16[2,256,512]{2,1,0:T(8,128)(2,1)S(1)} custom-call(s32[2]{0:T(128)} %cached_in.1, s32[2]{0:T(128)} %span_in.1, s32[2]{0:T(128)} %sinkn_in.1, s32[2]{0:T(128)} %reach_in.1, bf16[2,256,512]{2,1,0:T(8,128)(2,1)} %hid.1, f32[1,2048]{1,0:T(1,128)} %bitcast.2, bf16[2048,512]{1,0:T(8,128)(2,1)} %qw.1, bf16[2048,256]{1,0:T(8,128)(2,1)} %kvw.1, ...), custom_call_target="tpu_custom_call" | custom-call | tf_op jit(solution)/shard_map/pallas_call | solution.py:370
  41.5 0.8 %copy.14 = bf16[2,256,512]{2,1,0:T(8,128)(2,1)} copy(bf16[2,256,512]{2,1,0:T(8,128)(2,1)S(1)} %shard_map.118) | data formatting | bytes 1048576
